TPU v7x, 512 devices: a whole 4x8x8 slice. The times are simulated.
512 devices in a mesh: occ: 128 (over z_lo, x, y), grp: 4 (over z_hi, core).
Axes of the slice: x: 4, y: 8, z: 8 (z_hi: 2, z_lo: 4; z = z_hi * 4 + z_lo), core: 2. Of those that a mesh axis runs over, the one named last changes fastest.
Arguments:
- slabs: float32 [512, 512, 1024], P(('occ', 'grp')), may hold values from -4 to 4
- occ_energy: float32 [512], replicated, may hold values from -1.5 to -0.3
- vir_energy: float32 [512], replicated, may hold values from 0.1 to 3
- pair_mask: int32 [512, 2], replicated, may hold values from 0 to 1, as said below
Outputs:
- aux_grad: float32 [512, 512, 1024], P(('occ', 'grp'))
- vir_density: float32 [512, 512], P('occ')
Inputs may be any that keep to these rules, and one draw needn't show every extreme that they name: Entries are 0 or 1; orbital 0 is paired with all of its 2 partners, and so is every orbital i >= 512 - 1 - 2 (pair_mask[i, k - 1] = 1 for every 1 <= k <= 2 on those rows).
All inputs are finite; a program needn't handle non-finite values.
Results may differ from a plain program's by a relative error of at most 0.0003.
Values sent between devices are 32-bit elements; how exact they have to be, the bound alone decides.
A program may use at most 128 MiB of HBM per device.

v0:
```python
import jax
import jax.numpy as jnp
from jax import lax
from jax.sharding import PartitionSpec as P

highest = lax.Precision.HIGHEST


def shifted(block, axis, distance):
    devices = range(lax.axis_size(axis))
    route = [(i - distance, i) for i in devices if i - distance in devices]
    return lax.ppermute(block, axis, route)


def pair_terms(left_slab, right_slab, left_energy, right_energy, virtual):
    coulomb = jnp.dot(
        left_slab, right_slab.T, precision=highest, preferred_element_type=jnp.float32
    )
    denominator = left_energy + right_energy - virtual[:, None] - virtual[None, :]
    amplitude = coulomb / denominator
    grad_left = jnp.dot(
        amplitude, right_slab, precision=highest, preferred_element_type=jnp.float32
    )
    grad_right = jnp.dot(
        amplitude.T, left_slab, precision=highest, preferred_element_type=jnp.float32
    )
    density = jnp.dot(amplitude, amplitude.T, precision=highest, preferred_element_type=jnp.float32)
    density = density + jnp.dot(
        amplitude.T, amplitude, precision=highest, preferred_element_type=jnp.float32
    )
    return (grad_left, grad_right, density)


def body(slabs, occ_energy, vir_energy, pair_mask):
    own_slab = slabs[0]
    orbitals = lax.axis_size(("occ", "grp"))
    position = lax.axis_index(("occ", "grp"))
    own_energy = lax.dynamic_index_in_dim(occ_energy, position, 0, keepdims=False)
    grad_left, grad_right, density = pair_terms(
        own_slab, own_slab, own_energy, own_energy, vir_energy
    )
    gradient = grad_left + grad_right
    offsets = pair_mask.shape[1]
    for offset in range(1, offsets + 1):
        column = pair_mask[:, offset - 1]
        partner_index = jnp.minimum(position + offset, orbitals - 1)
        partner_energy = lax.dynamic_index_in_dim(occ_energy, partner_index, 0, keepdims=False)
        forward_flag = lax.dynamic_index_in_dim(column, position, 0, keepdims=False)
        forward_active = (forward_flag == 1) & (position + offset < orbitals)
        partner_slab = shifted(own_slab, ("occ", "grp"), -offset)

        def whole_pair():
            return pair_terms(own_slab, partner_slab, own_energy, partner_energy, vir_energy)

        def empty_pair():
            return (jnp.zeros_like(own_slab), jnp.zeros_like(own_slab), jnp.zeros_like(density))

        grad_left, grad_right, term = lax.cond(forward_active, whole_pair, empty_pair)
        returned = shifted(grad_right, ("occ", "grp"), offset)
        gradient = gradient + grad_left + returned
        density = density + term
    row_count = density.shape[0] // lax.axis_size("occ")
    summed = lax.psum(density, ("occ", "grp"))
    own_rows = lax.dynamic_slice_in_dim(summed, lax.axis_index("occ") * row_count, row_count, 0)
    return (gradient[None], own_rows / orbitals)


def solution(mesh):
    placed = (P(("occ", "grp"), None, None), P(), P(), P())
    return jax.shard_map(
        body,
        mesh=mesh,
        in_specs=placed,
        out_specs=(P(("occ", "grp"), None, None), P("occ", None)),
        check_vma=False,
    )
```

profile of v0, /device:TPU:24, one launch (start us, length us, event | category | flops | bytes accessed | tf_op | source)
XLA Modules:
  0.0 632.4 jit_solution(11234347557603762785)
XLA Ops:
  7.2 0.0 all-reduce.2.cloned.1.call-start
  7.2 10.2 %collective-permute-start = (f32[512,1024]{1,0:T(8,128)}, f32[512,1024]{1,0:T(8,128)S(1)}, u32[]{:S(2)}, u32[]{:S(2)}) collective-permute-start(f32[512,1024]{1,0:T(8,128)} %bitcast.34), channel_id=1, source_target_pairs={{1,0},{2,1},{3,2},{4,3},{5,4},{6,5},{7,6},{8,7},{9,8},{10,9},{11,1... | collective-permute-start | bytes 6291464 | tf_op jit(solution)/shard_map/ppermute | solution.py:12
  17.5 2.5 collective-permute-start.2
  20.0 1.3 dynamic_slice.24
  21.2 0.8 fusion.27
  22.0 0.6 fusion.28
  25.2 72.1 %collective-permute-done = f32[512,1024]{1,0:T(8,128)S(1)} collective-permute-done((f32[512,1024]{1,0:T(8,128)}, f32[512,1024]{1,0:T(8,128)S(1)}, u32[]{:S(2)}, u32[]{:S(2)}) %collective-permute-start) | collective-permute-done | bytes 2097184 | tf_op jit(solution)/shard_map/ppermute | solution.py:12
  97.2 2.2 conditional.2
  97.2 0.2 broadcast.20
  97.5 1.6 broadcast.20.clone
  99.1 0.1 broadcast.21
  99.4 0.0 copy-start.3
  99.4 4.8 collective-permute-start.1
  104.3 134.5 %collective-permute-done.2 = f32[512,1024]{1,0:T(8,128)} collective-permute-done((f32[512,1024]{1,0:T(8,128)}, f32[512,1024]{1,0:T(8,128)}, u32[]{:S(2)}, u32[]{:S(2)}) %collective-permute-start.2) | collective-permute-done | bytes 2097184 | tf_op jit(solution)/shard_map/ppermute | solution.py:12
  238.8 0.0 copy-done.3
  238.8 4.5 conditional.3
  238.8 1.6 broadcast.22
  240.4 1.6 broadcast.22.clone
  242.0 1.1 broadcast.23
  243.3 0.0 copy-start.8
  243.3 1.9 collective-permute-start.3
  245.2 0.7 broadcast_subtract_fusion.2
  245.9 5.7 fusion.25
  251.7 0.0 copy-done.8
  251.7 0.0 copy-start.4
  251.7 2.3 fusion
  254.0 0.0 copy-done.4
  254.0 2.2 fusion.12
  256.2 0.0 copy-start
  256.2 2.7 add_add_fusion
  258.9 0.0 all-reduce.2.cloned.1.call-update
  259.0 0.0 copy-done
  259.0 0.0 copy-start.5
  259.0 6.3 fusion.4
  265.3 0.0 copy-done.5
  265.3 5.2 fusion.6
  270.5 345.6 %all-reduce.2.cloned.1.call-done = f32[512,512]{1,0:T(8,128)} async-done(((f32[512,512]{1,0:T(8,128)}), f32[512,512]{1,0:T(8,128)}) %all-reduce.2.cloned.1.call-update) | async-done | bytes 1048592 | tf_op jit(solution)/shard_map/psum | solution.py:63
  616.1 1.3 dynamic-slice_multiply_fusion
  617.4 0.0 collective-permute-done.1
  617.4 0.0 collective-permute-done.3
  617.4 7.7 %add_bitcast_fusion = f32[1,512,1024]{2,1,0:T(8,128)} fusion(f32[512,1024]{1,0:T(8,128)} %collective-permute-done.3, f32[512,1024]{1,0:T(8,128)} %get-tuple-element.104, f32[512,1024]{1,0:T(8,128)} %collective-permute-done.1, f32[512,1024]{1,0:T(8,128)} %copy-done.3, f32[512,1024]{1,0:T(8,128)} %fusion.6, f32[512,1024]{1,0:T(8,128)} %fusion.4), kind=kLoop, calls=%fused_computation.6 | loop fusion | flops 2621440 | bytes 14680064 | tf_op jit(solution)/shard_map/broadcast_in_dim | solution.py:65
Async XLA Ops:
  7.2 608.9 %all-reduce.2.cloned.1.call-start = ((), (), s32[]{:S(2)}) async-start(), calls=%async_computation | async-start | bytes 2097152 | tf_op jit(solution)/shard_map/psum | solution.py:63
  7.2 90.0 %collective-permute-start = (f32[512,1024]{1,0:T(8,128)}, f32[512,1024]{1,0:T(8,128)S(1)}, u32[]{:S(2)}, u32[]{:S(2)}) collective-permute-start(f32[512,1024]{1,0:T(8,128)} %bitcast.34), channel_id=1, source_target_pairs={{1,0},{2,1},{3,2},{4,3},{5,4},{6,5},{7,6},{8,7},{9,8},{10,9},{11,1... | collective-permute-start | bytes 6291464 | tf_op jit(solution)/shard_map/ppermute | solution.py:12
  17.5 221.3 %collective-permute-start.2 = (f32[512,1024]{1,0:T(8,128)}, f32[512,1024]{1,0:T(8,128)}, u32[]{:S(2)}, u32[]{:S(2)}) collective-permute-start(f32[512,1024]{1,0:T(8,128)} %bitcast.35), channel_id=1, source_target_pairs={{2,0},{3,1},{4,2},{5,3},{6,4},{7,5},{8,6},{9,7},{10,8},{11,9},{12,... | collective-permute-start | bytes 6291464 | tf_op jit(solution)/shard_map/ppermute | solution.py:12
  99.4 139.4 %copy-start.3 = (f32[512,1024]{1,0:T(8,128)}, f32[512,1024]{1,0:T(8,128)S(1)}, u32[]{:S(2)}) copy-start(f32[512,1024]{1,0:T(8,128)S(1)} %get-tuple-element.102) | copy-start | bytes 6291460
  99.4 518.0 %collective-permute-start.1 = (f32[512,1024]{1,0:T(8,128)}, f32[512,1024]{1,0:T(8,128)}, u32[]{:S(2)}, u32[]{:S(2)}) collective-permute-start(f32[512,1024]{1,0:T(8,128)} %get-tuple-element.103), channel_id=1, source_target_pairs={{0,1},{1,2},{2,3},{3,4},{4,5},{5,6},{6,7},{7,8},{8,9},{9,10},{10,1... | collective-permute-start | bytes 6291464 | tf_op jit(solution)/shard_map/ppermute | solution.py:12
  243.3 8.4 %copy-start.8 = (f32[512]{0:T(512)S(1)}, f32[512]{0:T(512)}, u32[]{:S(2)}) copy-start(f32[512]{0:T(512)} %param.10) | copy-start | bytes 6148
  243.3 374.1 %collective-permute-start.3 = (f32[512,1024]{1,0:T(8,128)}, f32[512,1024]{1,0:T(8,128)}, u32[]{:S(2)}, u32[]{:S(2)}) collective-permute-start(f32[512,1024]{1,0:T(8,128)} %get-tuple-element.105), channel_id=1, source_target_pairs={{0,2},{1,3},{2,4},{3,5},{4,6},{5,7},{6,8},{7,9},{8,10},{9,11},{10,... | collective-permute-start | bytes 6291464 | tf_op jit(solution)/shard_map/ppermute | solution.py:12
  251.7 2.3 copy-start.4
  256.2 2.8 copy-start
  259.0 6.3 copy-start.5
Sparse Core Ops, SparseCore 0:
  259.1 356.9 all-reduce.1
where the time goes:
time: 643 us; the launch traced here: 632 us
  waiting for transfers between devices  552 us (86%)
  matrix products  21.8 us (3%)
  starting transfers between devices  19.5 us (3%)
  between operations  17.2 us (3%)
  other arithmetic  13 us (2%)
  local copies, waits for them, and re-layouts  8.33 us (1%)
    psum x1, waiting for transfers between devices, body(): summed = lax.psum(density, ('occ', 'grp'))  346 us
    ppermute x4, waiting for transfers between devices, shifted(): return lax.ppermute(block, axis, route)  207 us
    ppermute x4, starting transfers between devices, shifted(): return lax.ppermute(block, axis, route)  19.5 us
  transfers between devices with their start and end apart: 5, of which 3 were waited for; matrix products, arithmetic and copies ran while one was open for 6% of the time, Pallas kernels for 0%

commit v1 on v0

--- a/solution.py
+++ b/solution.py
@@ -60,7 +60,9 @@
         gradient = gradient + grad_left + returned
         density = density + term
     row_count = density.shape[0] // lax.axis_size("occ")
-    summed = lax.psum(density, ("occ", "grp"))
+    summed = density
+    for i0 in ("occ", "grp"):
+        summed = lax.psum(summed, i0)
     own_rows = lax.dynamic_slice_in_dim(summed, lax.axis_index("occ") * row_count, row_count, 0)
     return (gradient[None], own_rows / orbitals)
 

time: 643 us -> 1810 us (2.81)
  the two profiles are of different devices: /device:TPU:24 before, /device:TPU:1 now
where the time goes in v1:
time: 1810 us; the launch traced here: 1800 us
  waiting for transfers between devices  1650 us (91%)
  starting transfers between devices  62.4 us (3%)
  matrix products  42.3 us (2%)
    psum x2, waiting for transfers between devices, body(): summed = lax.psum(summed, i0)  1590 us
    ppermute x4, starting transfers between devices, shifted(): return lax.ppermute(block, axis, route)  62.3 us
    ppermute x4, waiting for transfers between devices, shifted(): return lax.ppermute(block, axis, route)  58.7 us
  transfers between devices with their start and end apart: 6, of which 4 were waited for; matrix products, arithmetic and copies ran while one was open for 2% of the time, Pallas kernels for 0%

profile of v1, /device:TPU:1, one launch (start us, length us, event | category | flops | bytes accessed | tf_op | source)
XLA Modules:
  0.0 1804.8 jit_solution(5705024909884368826)
XLA Ops:
  7.2 0.0 copy-start.3
  7.2 0.0 all-reduce.3.cloned.1.call-start
  7.2 8.8 collective-permute-start
  16.0 1.3 collective-permute-start.2
  17.3 1.3 dynamic_slice.24
  18.6 0.8 fusion.27
  19.4 0.6 fusion.28
  22.5 0.7 broadcast_subtract_fusion.2
  23.2 5.7 fusion.25
  29.0 0.0 copy-done.3
  29.0 0.0 copy-start.1
  29.0 2.3 fusion
  31.3 0.0 copy-done.1
  31.3 0.0 copy-start
  31.3 0.0 copy-start.4
  31.3 3.2 fusion.12
  34.5 58.2 %collective-permute-done = f32[512,1024]{1,0:T(8,128)} collective-permute-done((f32[512,1024]{1,0:T(8,128)}, f32[512,1024]{1,0:T(8,128)}, u32[]{:S(2)}, u32[]{:S(2)}) %collective-permute-start) | collective-permute-done | bytes 2097184 | tf_op jit(solution)/shard_map/ppermute | solution.py:12
  92.7 0.0 copy-done
  92.7 0.0 copy-done.4
  92.7 13.7 conditional.2
  92.7 1.6 broadcast.20
  94.4 1.6 broadcast.20.clone
  95.9 0.1 broadcast.21
  106.4 0.5 collective-permute-done.2
  106.9 23.2 %conditional.3 = (f32[512,1024]{1,0:T(8,128)}, f32[512,1024]{1,0:T(8,128)}, f32[512,512]{1,0:T(8,128)}) conditional(s32[]{:T(128)} %convert_element_type.7, () %tuple.32, (f32[512,1024]{1,0:T(8,128)S(1)}, f32[512,1024]{1,0:T(8,128)}, s32[]{:T(128)}, f32[512]{0:T(512)S(1)}, f32[]{:T(128)}, /*index=5*/f32[512]{0:T(512)S(1)}) %tuple.50), branch_computations={%region_2.3_spmd, %region_3.4_spmd} | conditional | flops 12885688320 | bytes 20979810 | solution.py:58
  106.9 0.6 dynamic_slice.19
  108.7 5.1 convolution_divide_fusion.1
  113.9 1.9 fusion.35
  115.8 2.9 convolution_add_fusion.1
  118.7 6.5 fusion.33
  125.1 4.8 fusion.34
  130.1 2.9 add_add_fusion
  133.0 0.0 copy-start.2
  133.0 0.0 all-reduce.3.cloned.1.call-update
  133.1 0.0 all-reduce.5.cloned.1.call-start
  133.1 49.7 %collective-permute-start.1 = (f32[512,1024]{1,0:T(8,128)}, f32[512,1024]{1,0:T(8,128)}, u32[]{:S(2)}, u32[]{:S(2)}) collective-permute-start(f32[512,1024]{1,0:T(8,128)} %get-tuple-element.103), channel_id=1, source_target_pairs={{0,1},{1,2},{2,3},{3,4},{4,5},{5,6},{6,7},{7,8},{8,9},{9,10},{10,1... | collective-permute-start | bytes 6291464 | tf_op jit(solution)/shard_map/ppermute | solution.py:12
  182.8 2.6 collective-permute-start.3
  185.4 1437.9 %all-reduce.3.cloned.1.call-done = f32[512,512]{1,0:T(8,128)} async-done(((f32[512,512]{1,0:T(8,128)}), f32[512,512]{1,0:T(8,128)}) %all-reduce.3.cloned.1.call-update) | async-done | bytes 1048592 | tf_op jit(solution)/shard_map/psum | solution.py:65
  1623.3 0.0 all-reduce.5.cloned.1.call-update
  1623.3 0.0 copy-done.2
  1623.4 5.0 fusion.4
  1628.3 4.9 fusion.6
  1633.3 155.5 %all-reduce.5.cloned.1.call-done = f32[512,512]{1,0:T(8,128)} async-done(((f32[512,512]{1,0:T(8,128)}), f32[512,512]{1,0:T(8,128)}) %all-reduce.5.cloned.1.call-update) | async-done | bytes 1048592 | tf_op jit(solution)/shard_map/psum | solution.py:65
  1788.7 1.3 dynamic-slice_multiply_fusion
  1790.0 0.0 collective-permute-done.1
  1790.0 0.0 collective-permute-done.3
  1790.0 7.7 add_bitcast_fusion
  (1 shorter events, 0.0 us)
Async XLA Ops:
  7.2 21.8 %copy-start.3 = (f32[512]{0:T(512)S(1)}, f32[512]{0:T(512)}, u32[]{:S(2)}) copy-start(f32[512]{0:T(512)} %param.10) | copy-start | bytes 6148
  7.2 1616.2 %all-reduce.3.cloned.1.call-start = ((), (), s32[]{:S(2)}) async-start(), calls=%async_computation | async-start | bytes 2097152 | tf_op jit(solution)/shard_map/psum | solution.py:65
  7.2 85.5 %collective-permute-start = (f32[512,1024]{1,0:T(8,128)}, f32[512,1024]{1,0:T(8,128)}, u32[]{:S(2)}, u32[]{:S(2)}) collective-permute-start(f32[512,1024]{1,0:T(8,128)} %bitcast.34), channel_id=1, source_target_pairs={{1,0},{2,1},{3,2},{4,3},{5,4},{6,5},{7,6},{8,7},{9,8},{10,9},{11,1... | collective-permute-start | bytes 6291464 | tf_op jit(solution)/shard_map/ppermute | solution.py:12
  16.0 90.9 %collective-permute-start.2 = (f32[512,1024]{1,0:T(8,128)}, f32[512,1024]{1,0:T(8,128)}, u32[]{:S(2)}, u32[]{:S(2)}) collective-permute-start(f32[512,1024]{1,0:T(8,128)} %bitcast.35), channel_id=1, source_target_pairs={{2,0},{3,1},{4,2},{5,3},{6,4},{7,5},{8,6},{9,7},{10,8},{11,9},{12,... | collective-permute-start | bytes 6291464 | tf_op jit(solution)/shard_map/ppermute | solution.py:12
  29.0 2.3 copy-start.1
  31.3 61.4 %copy-start = (f32[1,512,1024]{2,1,0:T(8,128)S(1)}, f32[1,512,1024]{2,1,0:T(8,128)}, u32[]{:S(2)}) copy-start(f32[1,512,1024]{2,1,0:T(8,128)} %param.8) | copy-start | bytes 6291460
  31.3 61.4 %copy-start.4 = (f32[512]{0:T(512)S(1)}, f32[512]{0:T(512)}, u32[]{:S(2)}) copy-start(f32[512]{0:T(512)} %param.9) | copy-start | bytes 6148
  133.0 1490.3 %copy-start.2 = (f32[512,512]{1,0:T(8,128)S(1)}, f32[512,512]{1,0:T(8,128)}, u32[]{:S(2)}) copy-start(f32[512,512]{1,0:T(8,128)} %copy-done.1) | copy-start | bytes 3145732
  133.1 1655.7 %all-reduce.5.cloned.1.call-start = ((), (), s32[]{:S(2)}) async-start(), calls=%async_computation.1 | async-start | bytes 2097152 | tf_op jit(solution)/shard_map/psum | solution.py:65
  133.1 1656.9 %collective-permute-start.1 = (f32[512,1024]{1,0:T(8,128)}, f32[512,1024]{1,0:T(8,128)}, u32[]{:S(2)}, u32[]{:S(2)}) collective-permute-start(f32[512,1024]{1,0:T(8,128)} %get-tuple-element.103), channel_id=1, source_target_pairs={{0,1},{1,2},{2,3},{3,4},{4,5},{5,6},{6,7},{7,8},{8,9},{9,10},{10,1... | collective-permute-start | bytes 6291464 | tf_op jit(solution)/shard_map/ppermute | solution.py:12
  182.8 1607.3 %collective-permute-start.3 = (f32[512,1024]{1,0:T(8,128)}, f32[512,1024]{1,0:T(8,128)}, u32[]{:S(2)}, u32[]{:S(2)}) collective-permute-start(f32[512,1024]{1,0:T(8,128)} %get-tuple-element.105), channel_id=1, source_target_pairs={{0,2},{1,3},{2,4},{3,5},{4,6},{5,7},{6,8},{7,9},{8,10},{9,11},{10,... | collective-permute-start | bytes 6291464 | tf_op jit(solution)/shard_map/ppermute | solution.py:12
Sparse Core Ops, SparseCore 0:
  133.2 1490.1 all-reduce.2
  1626.3 162.3 all-reduce.4
